TPU v7x, 32 devices: a whole 2x2x4 slice. The times are simulated.
32 devices in a mesh: seq: 8 (over z, y), head: 4 (over x, core).
Axes of the slice: x: 2, y: 2, z: 4, core: 2. Of those that a mesh axis runs over, the one named last changes fastest.
Arguments:
- queries: bfloat16 [1024, 4096], P(('seq', 'head')), may hold values from -6 to 6
- keys: bfloat16 [1024, 4096], P(('seq', 'head')), may hold values from -0.5 to 0.5
- values: bfloat16 [1024, 4096], P(('seq', 'head')), may hold values from -6 to 6
- log_decay: float32 [1024, 32], P('seq', 'head'), may hold values from -2 to 0, as said below
- out_grad: bfloat16 [1024, 4096], P('seq', 'head'), may hold values from -6 to 6
Outputs:
- attn_out: bfloat16 [1024, 4096], P('seq', 'head')
- query_grad: bfloat16 [1024, 4096], P('seq', 'head')
- key_grad: bfloat16 [1024, 4096], P('seq', 'head')
- value_grad: bfloat16 [1024, 4096], P('seq', 'head')
Inputs may be any that keep to these rules, and one draw needn't show every extreme that they name: `log_decay`: never positive.
All inputs are finite; a program needn't handle non-finite values.
Results may differ from a plain program's by a relative error of at most 0.0056.
Values may be sent and summed in bfloat16 or wider, within the bound.
No kernel may reach another device: no remote copies, remote signals or barrier semaphores. Data moves between devices by JAX's collectives and lax.ppermute only.
A program may use at most 64 MiB of HBM per device.

v0:
```python
import jax
import jax.numpy as jnp
from jax import lax
from jax.sharding import PartitionSpec as P

DK = 128
split_mode = lax.Precision.HIGH


def prefix(array, axis, combine, identity, reverse):
    length, index = (lax.axis_size(axis), lax.axis_index(axis))
    everything = jax.tree.map(lambda part: lax.all_gather(part, axis), array)
    start = jax.tree.map(
        lambda part, zero: jnp.broadcast_to(jnp.asarray(zero, part.dtype), part.shape),
        array,
        identity,
    )

    def lap(k, before):
        at = length - 1 - k if reverse else k
        reached = at > index if reverse else at < index
        new = combine(before, jax.tree.map(lambda part: part[at], everything))
        return jax.tree.map(lambda a, b: jnp.where(reached, a, b), new, before)

    return lax.fori_loop(0, length, lap, start)


def decay_table(running):
    block_rows = running.shape[0]
    gaps = running.T[:, :, None] - running.T[:, None, :]
    causal = lax.broadcasted_iota(jnp.int32, (block_rows, block_rows), 0) >= lax.broadcasted_iota(
        jnp.int32, (block_rows, block_rows), 1
    )
    return jnp.where(causal[None], jnp.exp(jnp.where(causal[None], gaps, 0.0)), 0.0)


def chained(earlier, later):
    return (earlier[0] * later[0], later[0][:, None, None] * earlier[1] + later[1])


def pass_states(factor, own_state):
    identity = (jnp.ones_like(factor), jnp.zeros_like(own_state))
    return prefix((factor, own_state), "seq", chained, identity, False)[1]


def pass_gradients(factor, own_grad):
    identity = (jnp.ones_like(factor), jnp.zeros_like(own_grad))
    return prefix((factor, own_grad), "seq", chained, identity, True)[1]


def local(queries, keys, values, log_decay, out_grad):
    block_rows = log_decay.shape[0]
    head_count = log_decay.shape[1]
    layout = (block_rows, head_count, DK)
    running = jnp.cumsum(log_decay, axis=0)
    final = running[-1]
    factor = jnp.exp(final)
    rising = jnp.exp(running)[:, :, None]
    tail_weight = jnp.exp(final[None, :] - running)[:, :, None]
    query_all, key_all, value_all = (
        lax.all_to_all(queries, "head", split_axis=1, concat_axis=0, tiled=True),
        lax.all_to_all(keys, "head", split_axis=1, concat_axis=0, tiled=True),
        lax.all_to_all(values, "head", split_axis=1, concat_axis=0, tiled=True),
    )
    key_rows = key_all.reshape(layout)
    value_rows = value_all.reshape(layout)
    key_wide = key_rows.astype(jnp.float32)
    state_in = pass_states(
        factor,
        jnp.einsum(
            "thd,the->hde",
            key_wide * tail_weight,
            value_rows.astype(jnp.float32),
            precision=split_mode,
        ),
    )
    query_rows = query_all.reshape(layout)
    table = decay_table(running)
    query_wide = query_rows.astype(jnp.float32)
    scores = jnp.einsum("thd,shd->hts", query_rows, key_rows, preferred_element_type=jnp.float32)
    weighted = (scores * table).astype(jnp.bfloat16)
    inner = jnp.einsum("hts,she->the", weighted, value_rows, preferred_element_type=jnp.float32)
    mixed = inner + rising * jnp.einsum("thd,hde->the", query_wide, state_in, precision=split_mode)
    inverse = lax.rsqrt(jnp.mean(mixed * mixed, axis=-1) + 1e-06)[:, :, None]
    normed = mixed * inverse
    grad_wide = out_grad.reshape(layout).astype(jnp.float32)
    out_delta = (
        inverse * (grad_wide - normed * jnp.mean(grad_wide * normed, axis=-1, keepdims=True))
    ).astype(jnp.bfloat16)
    delta_wide = out_delta.astype(jnp.float32)
    own_grad = jnp.einsum("thd,the->hde", query_wide * rising, delta_wide, precision=split_mode)
    grad_state = pass_gradients(factor, own_grad)
    delta_scores = jnp.einsum(
        "the,she->hts", out_delta, value_rows, preferred_element_type=jnp.float32
    )
    delta_weighted = (delta_scores * table).astype(jnp.bfloat16)
    query_grad = jnp.einsum(
        "hts,shd->thd", delta_weighted, key_rows, preferred_element_type=jnp.float32
    )
    query_grad = query_grad + rising * jnp.einsum(
        "the,hde->thd", delta_wide, state_in, precision=split_mode
    )
    key_grad = jnp.einsum(
        "hts,thd->shd", delta_weighted, query_rows, preferred_element_type=jnp.float32
    )
    key_grad = key_grad + tail_weight * jnp.einsum(
        "she,hde->shd", value_rows.astype(jnp.float32), grad_state, precision=split_mode
    )
    value_grad = jnp.einsum("hts,the->she", weighted, out_delta, preferred_element_type=jnp.float32)
    value_grad = value_grad + tail_weight * jnp.einsum(
        "shd,hde->she", key_rows.astype(jnp.float32), grad_state, precision=split_mode
    )
    flat = (block_rows, head_count * DK)
    return (
        normed.astype(jnp.bfloat16).reshape(flat),
        query_grad.astype(jnp.bfloat16).reshape(flat),
        key_grad.astype(jnp.bfloat16).reshape(flat),
        value_grad.astype(jnp.bfloat16).reshape(flat),
    )


def solution(mesh):
    placed = (
        P(("seq", "head"), None),
        P(("seq", "head"), None),
        P(("seq", "head"), None),
        P("seq", "head"),
        P("seq", "head"),
    )
    return jax.shard_map(
        local,
        mesh=mesh,
        in_specs=placed,
        out_specs=(P("seq", "head"), P("seq", "head"), P("seq", "head"), P("seq", "head")),
        check_vma=False,
    )
```

profile of v0, /device:TPU:0, one launch (start us, length us, event | category | flops | bytes accessed | tf_op | source)
XLA Modules:
  0.0 206.9 jit_solution(703860958930601982)
XLA Ops:
  7.2 1.7 copy.122
  8.9 4.2 %all-to-all-start.1 = ((bf16[32,4,1024]{2,0,1:T(8,128)(2,1)}), bf16[32,4,1024]{2,0,1:T(8,128)(2,1)S(1)}, u32[]{:S(2)}, u32[]{:S(2)}) async-start(bf16[32,4,1024]{2,0,1:T(8,128)(2,1)} %bitcast.104), calls=%async_computation.1 | async-start | bytes 524288 | tf_op jit(solution)/shard_map/all_to_all | solution.py:62
  13.9 1.7 copy.121
  15.8 3.4 %all-to-all-done.1 = bf16[32,4,1024]{2,0,1:T(8,128)(2,1)S(1)} async-done(((bf16[32,4,1024]{2,0,1:T(8,128)(2,1)}), bf16[32,4,1024]{2,0,1:T(8,128)(2,1)S(1)}, u32[]{:S(2)}, u32[]{:S(2)}) %all-to-all-start.1) | async-done | bytes 262176 | tf_op jit(solution)/shard_map/all_to_all | solution.py:62
  19.2 3.4 %all-to-all-start.2 = ((bf16[32,4,1024]{2,0,1:T(8,128)(2,1)}), bf16[32,4,1024]{2,0,1:T(8,128)(2,1)S(1)}, u32[]{:S(2)}, u32[]{:S(2)}) async-start(bf16[32,4,1024]{2,0,1:T(8,128)(2,1)} %bitcast.103), calls=%async_computation.2 | async-start | bytes 524288 | tf_op jit(solution)/shard_map/all_to_all | solution.py:63
  23.0 5.5 %all-to-all-done.2 = bf16[32,4,1024]{2,0,1:T(8,128)(2,1)S(1)} async-done(((bf16[32,4,1024]{2,0,1:T(8,128)(2,1)}), bf16[32,4,1024]{2,0,1:T(8,128)(2,1)S(1)}, u32[]{:S(2)}, u32[]{:S(2)}) %all-to-all-start.2) | async-done | bytes 262176 | tf_op jit(solution)/shard_map/all_to_all | solution.py:63
  30.4 3.4 %all-to-all-start = ((bf16[32,4,1024]{2,0,1:T(8,128)(2,1)}), bf16[32,4,1024]{2,0,1:T(8,128)(2,1)S(1)}, u32[]{:S(2)}, u32[]{:S(2)}) async-start(bf16[32,4,1024]{2,0,1:T(8,128)(2,1)} %bitcast.105), calls=%async_computation | async-start | bytes 524288 | tf_op jit(solution)/shard_map/all_to_all | solution.py:61
  34.2 21.9 %all-gather.2 = f32[8,1,8]{2,1,0:T(1,128)S(1)} all-gather(f32[1,1,8]{2,1,0:T(1,128)S(1)} %get-tuple-element.301), channel_id=1, replica_groups=mesh['seq'=8,'head'=4] {'seq'}, dimensions={0}, use_global_device_ids=true | all-gather | bytes 288 | tf_op jit(solution)/shard_map/all_gather | solution.py:12
  56.8 46.8 %all-gather.6.cloned.1.call-done = f32[64,128,128]{2,1,0:T(8,128)} async-done(((f32[8,128,128]{2,1,0:T(8,128)}), f32[64,128,128]{2,1,0:T(8,128)}) %all-gather.6.cloned.1.call-update) | async-done | bytes 4194320 | tf_op jit(solution)/shard_map/all_gather | solution.py:12
  103.6 9.7 %while.30 = (s32[]{:T(128)}, f32[8,128,128]{2,1,0:T(8,128)S(1)}, s32[]{:T(128)}, f32[8,8]{1,0:T(8,128)S(1)}, f32[8,8,128,128]{3,2,1,0:T(8,128)}, /*index=5*/s32[]{:T(128)}, s32[]{:T(128)}) while((s32[]{:T(128)}, f32[8,128,128]{2,1,0:T(8,128)S(1)}, s32[]{:T(128)}, f32[8,8]{1,0:T(8,128)S(1)}, f32[8,8,128,128]{3,2,1,0:T(8,128)}, ...), condition=%wide.region_2.3_spmd.clone, body=%wide.region_1.2_spmd.clone.sunk | while | flops 524292 | bytes 1573073 | solution.py:25
  104.8 1.2 fusion.51
  108.5 1.2 fusion.51
  109.7 1.2 fusion.51
  110.9 1.2 fusion.51
  114.4 1.3 fusion.18
  118.3 68.8 %all-gather.8.cloned.1.call-done = f32[64,128,128]{2,1,0:T(8,128)} async-done(((f32[8,128,128]{2,1,0:T(8,128)}), f32[64,128,128]{2,1,0:T(8,128)}) %all-gather.8.cloned.1.call-update) | async-done | bytes 4194320 | tf_op jit(solution)/shard_map/all_gather | solution.py:12
  187.2 9.8 %while.31 = (s32[]{:T(128)}, f32[8,128,128]{2,1,0:T(8,128)S(1)}, s32[]{:T(128)}, f32[8,8]{1,0:T(8,128)S(1)}, f32[8,8,128,128]{3,2,1,0:T(8,128)}, /*index=5*/s32[]{:T(128)}, s32[]{:T(128)}, s32[]{:T(128)}, s32[]{:T(128)}) while((s32[]{:T(128)}, f32[8,128,128]{2,1,0:T(8,128)S(1)}, s32[]{:T(128)}, f32[8,8]{1,0:T(8,128)S(1)}, ...), condition=%wide.region_6.7_spmd.clone, body=%wide.region_5.6_spmd.clone.sunk | while | flops 524296 | bytes 1573135 | solution.py:25
  188.4 1.2 fusion.52
  189.6 1.2 fusion.52
  190.8 1.2 fusion.52
  192.1 1.2 fusion.52
  193.3 1.2 fusion.52
  194.5 1.2 fusion.52
  195.7 1.2 fusion.52
  (66 shorter events, 16.9 us)
Async XLA Ops:
  7.2 22.5 %copy-start = (bf16[32,4096]{1,0:T(8,128)(2,1)S(1)}, bf16[32,4096]{1,0:T(8,128)(2,1)}, u32[]{:S(2)}) copy-start(bf16[32,4096]{1,0:T(8,128)(2,1)} %param.9) | copy-start | bytes 786436
  7.2 26.9 %copy-start.1 = (bf16[128,1024]{1,0:T(8,128)(2,1)S(1)}, bf16[128,1024]{1,0:T(8,128)(2,1)}, u32[]{:S(2)}) copy-start(bf16[128,1024]{1,0:T(8,128)(2,1)} %param.13) | copy-start | bytes 786436
  8.9 10.2 %all-to-all-start.1 = ((bf16[32,4,1024]{2,0,1:T(8,128)(2,1)}), bf16[32,4,1024]{2,0,1:T(8,128)(2,1)S(1)}, u32[]{:S(2)}, u32[]{:S(2)}) async-start(bf16[32,4,1024]{2,0,1:T(8,128)(2,1)} %bitcast.104), calls=%async_computation.1 | async-start | bytes 524288 | tf_op jit(solution)/shard_map/all_to_all | solution.py:62
  19.2 9.4 %all-to-all-start.2 = ((bf16[32,4,1024]{2,0,1:T(8,128)(2,1)}), bf16[32,4,1024]{2,0,1:T(8,128)(2,1)S(1)}, u32[]{:S(2)}, u32[]{:S(2)}) async-start(bf16[32,4,1024]{2,0,1:T(8,128)(2,1)} %bitcast.103), calls=%async_computation.2 | async-start | bytes 524288 | tf_op jit(solution)/shard_map/all_to_all | solution.py:63
  22.6 81.1 %all-gather.6.cloned.1.call-start = ((), (), s32[]{:S(2)}) async-start(), calls=%async_computation.3 | async-start | bytes 4718592 | tf_op jit(solution)/shard_map/all_gather | solution.py:12
  30.4 25.7 %all-to-all-start = ((bf16[32,4,1024]{2,0,1:T(8,128)(2,1)}), bf16[32,4,1024]{2,0,1:T(8,128)(2,1)S(1)}, u32[]{:S(2)}, u32[]{:S(2)}) async-start(bf16[32,4,1024]{2,0,1:T(8,128)(2,1)} %bitcast.105), calls=%async_computation | async-start | bytes 524288 | tf_op jit(solution)/shard_map/all_to_all | solution.py:61
  33.9 153.3 %all-gather.8.cloned.1.call-start = ((), (), s32[]{:S(2)}) async-start(), calls=%async_computation.4 | async-start | bytes 4718592 | tf_op jit(solution)/shard_map/all_gather | solution.py:12
Sparse Core Ops, SparseCore 0:
  29.8 73.7 all-gather.5
  115.8 71.3 all-gather.7
where the time goes:
time: 208 us; the launch traced here: 207 us
  waiting for transfers between devices  125 us (60%)
  blocking collectives  21.9 us (11%)
  other arithmetic  19.2 us (9%)
  between operations  14.3 us (7%)
  starting transfers between devices  11.1 us (5%)
  local copies, waits for them, and re-layouts  9.4 us (5%)
  matrix products  5.79 us (3%)
    all_gather x2, waiting for transfers between devices, prefix(): everything = jax.tree.map(lambda part: lax.all_gather(part, axis), array)  116 us
    all_gather x1, blocking collectives, prefix(): everything = jax.tree.map(lambda part: lax.all_gather(part, axis), array)  21.9 us
    select_n x16, other arithmetic, lap(): return jax.tree.map(lambda a, b: jnp.where(reached, a, b), new, before)  18.8 us
    all_to_all x1, waiting for transfers between devices, local(): lax.all_to_all(values, 'head', split_axis=1, concat_axis=0, tiled=True)  5.53 us
    unnamed x13, local copies, waits for them, and re-layouts  4.54 us
    all_to_all x1, starting transfers between devices, local(): lax.all_to_all(keys, 'head', split_axis=1, concat_axis=0, tiled=True)  4.24 us
  transfers between devices with their start and end apart: 5, of which 4 were waited for; matrix products, arithmetic and copies ran while one was open for 4% of the time, Pallas kernels for 0%

commit v1 on v0

--- a/solution.py
+++ b/solution.py
@@ -57,10 +57,19 @@
     factor = jnp.exp(final)
     rising = jnp.exp(running)[:, :, None]
     tail_weight = jnp.exp(final[None, :] - running)[:, :, None]
+    match_tokens = lambda content, which_dim, shard_axis, array_axis: jnp.concatenate(
+        lax.all_to_all(
+            jnp.stack(jnp.split(content, lax.axis_size(shard_axis), which_dim), 0),
+            axis_name=shard_axis,
+            split_axis=0,
+            concat_axis=0,
+        ),
+        array_axis,
+    )
     query_all, key_all, value_all = (
         lax.all_to_all(queries, "head", split_axis=1, concat_axis=0, tiled=True),
         lax.all_to_all(keys, "head", split_axis=1, concat_axis=0, tiled=True),
-        lax.all_to_all(values, "head", split_axis=1, concat_axis=0, tiled=True),
+        match_tokens(values, 1, shard_axis="head", array_axis=0),
     )
     key_rows = key_all.reshape(layout)
     value_rows = value_all.reshape(layout)

time: 208 us -> 208 us (level)
  no operation moved by 1% of the time
where the time goes in v1:
time: 208 us; the launch traced here: 207 us
  waiting for transfers between devices  125 us (60%)
  blocking collectives  21.9 us (11%)
  other arithmetic  20 us (10%)
  between operations  14.3 us (7%)
  starting transfers between devices  11.1 us (5%)
  local copies, waits for them, and re-layouts  8.68 us (4%)
  matrix products  5.8 us (3%)
    all_gather x2, waiting for transfers between devices, prefix(): everything = jax.tree.map(lambda part: lax.all_gather(part, axis), array)  116 us
    all_gather x1, blocking collectives, prefix(): everything = jax.tree.map(lambda part: lax.all_gather(part, axis), array)  21.9 us
    select_n x16, other arithmetic, lap(): return jax.tree.map(lambda a, b: jnp.where(reached, a, b), new, before)  18.8 us
    all_to_all x1, waiting for transfers between devices, local(): lax.all_to_all(jnp.stack(jnp.split(content, lax.axis_size(shard_axis), wh...  5.53 us
    unnamed x13, local copies, waits for them, and re-layouts  4.54 us
    all_to_all x1, starting transfers between devices, local(): lax.all_to_all(keys, 'head', split_axis=1, concat_axis=0, tiled=True)  4.24 us
  transfers between devices with their start and end apart: 5, of which 4 were waited for; matrix products, arithmetic and copies ran while one was open for 4% of the time, Pallas kernels for 0%

profile of v1, /device:TPU:0, one launch (start us, length us, event | category | flops | bytes accessed | tf_op | source)
XLA Modules:
  0.0 206.9 jit_solution(9501611129364948338)
XLA Ops:
  7.2 1.7 copy.117
  8.9 4.2 %all-to-all-start.2 = ((bf16[32,4,1024]{2,0,1:T(8,128)(2,1)}), bf16[32,4,1024]{2,0,1:T(8,128)(2,1)S(1)}, u32[]{:S(2)}, u32[]{:S(2)}) async-start(bf16[32,4,1024]{2,0,1:T(8,128)(2,1)} %bitcast.107), calls=%async_computation.2 | async-start | bytes 524288 | tf_op jit(solution)/shard_map/all_to_all | solution.py:71
  15.8 3.3 %all-to-all-done.2 = bf16[32,4,1024]{2,0,1:T(8,128)(2,1)S(1)} async-done(((bf16[32,4,1024]{2,0,1:T(8,128)(2,1)}), bf16[32,4,1024]{2,0,1:T(8,128)(2,1)S(1)}, u32[]{:S(2)}, u32[]{:S(2)}) %all-to-all-start.2) | async-done | bytes 262176 | tf_op jit(solution)/shard_map/all_to_all | solution.py:71
  19.2 3.4 %all-to-all-start = ((bf16[4,32,1024]{2,1,0:T(8,128)(2,1)}), bf16[4,32,1024]{2,1,0:T(8,128)(2,1)S(1)}, u32[]{:S(2)}, u32[]{:S(2)}) async-start(bf16[4,32,1024]{2,1,0:T(8,128)(2,1)} %pad_maximum_fusion), calls=%async_computation | async-start | bytes 524288 | tf_op jit(solution)/shard_map/all_to_all | solution.py:61
  23.0 5.5 %all-to-all-done = bf16[4,32,1024]{2,1,0:T(8,128)(2,1)S(1)} async-done(((bf16[4,32,1024]{2,1,0:T(8,128)(2,1)}), bf16[4,32,1024]{2,1,0:T(8,128)(2,1)S(1)}, u32[]{:S(2)}, u32[]{:S(2)}) %all-to-all-start) | async-done | bytes 262176 | tf_op jit(solution)/shard_map/all_to_all | solution.py:61
  30.4 3.4 %all-to-all-start.1 = ((bf16[32,4,1024]{2,0,1:T(8,128)(2,1)}), bf16[32,4,1024]{2,0,1:T(8,128)(2,1)S(1)}, u32[]{:S(2)}, u32[]{:S(2)}) async-start(bf16[32,4,1024]{2,0,1:T(8,128)(2,1)} %bitcast.108), calls=%async_computation.1 | async-start | bytes 524288 | tf_op jit(solution)/shard_map/all_to_all | solution.py:70
  34.2 21.9 %all-gather.2 = f32[8,1,8]{2,1,0:T(1,128)S(1)} all-gather(f32[1,1,8]{2,1,0:T(1,128)S(1)} %get-tuple-element.305), channel_id=1, replica_groups=mesh['seq'=8,'head'=4] {'seq'}, dimensions={0}, use_global_device_ids=true | all-gather | bytes 288 | tf_op jit(solution)/shard_map/all_gather | solution.py:12
  56.8 46.8 %all-gather.6.cloned.1.call-done = f32[64,128,128]{2,1,0:T(8,128)} async-done(((f32[8,128,128]{2,1,0:T(8,128)}), f32[64,128,128]{2,1,0:T(8,128)}) %all-gather.6.cloned.1.call-update) | async-done | bytes 4194320 | tf_op jit(solution)/shard_map/all_gather | solution.py:12
  103.6 9.7 %while.30 = (s32[]{:T(128)}, f32[8,128,128]{2,1,0:T(8,128)S(1)}, s32[]{:T(128)}, f32[8,8]{1,0:T(8,128)S(1)}, f32[8,8,128,128]{3,2,1,0:T(8,128)}, /*index=5*/s32[]{:T(128)}, s32[]{:T(128)}) while((s32[]{:T(128)}, f32[8,128,128]{2,1,0:T(8,128)S(1)}, s32[]{:T(128)}, f32[8,8]{1,0:T(8,128)S(1)}, f32[8,8,128,128]{3,2,1,0:T(8,128)}, ...), condition=%wide.region_2.3_spmd.clone, body=%wide.region_1.2_spmd.clone.sunk | while | flops 524292 | bytes 1573073 | solution.py:25
  104.8 1.2 fusion.51
  106.1 1.2 fusion.51
  109.7 1.2 fusion.51
  110.9 1.2 fusion.51
  112.1 1.2 fusion.51
  114.4 1.3 fusion.18
  118.3 68.8 %all-gather.8.cloned.1.call-done = f32[64,128,128]{2,1,0:T(8,128)} async-done(((f32[8,128,128]{2,1,0:T(8,128)}), f32[64,128,128]{2,1,0:T(8,128)}) %all-gather.8.cloned.1.call-update) | async-done | bytes 4194320 | tf_op jit(solution)/shard_map/all_gather | solution.py:12
  187.2 9.8 %while.31 = (s32[]{:T(128)}, f32[8,128,128]{2,1,0:T(8,128)S(1)}, s32[]{:T(128)}, f32[8,8]{1,0:T(8,128)S(1)}, f32[8,8,128,128]{3,2,1,0:T(8,128)}, /*index=5*/s32[]{:T(128)}, s32[]{:T(128)}, s32[]{:T(128)}, s32[]{:T(128)}) while((s32[]{:T(128)}, f32[8,128,128]{2,1,0:T(8,128)S(1)}, s32[]{:T(128)}, f32[8,8]{1,0:T(8,128)S(1)}, ...), condition=%wide.region_6.7_spmd.clone, body=%wide.region_5.6_spmd.clone.sunk | while | flops 524296 | bytes 1573135 | solution.py:25
  188.4 1.2 fusion.52
  189.6 1.2 fusion.52
  190.8 1.2 fusion.52
  192.1 1.2 fusion.52
  193.3 1.2 fusion.52
  194.5 1.2 fusion.52
  195.7 1.2 fusion.52
  (67 shorter events, 17.5 us)
Async XLA Ops:
  7.2 22.5 %copy-start = (bf16[32,4096]{1,0:T(8,128)(2,1)S(1)}, bf16[32,4096]{1,0:T(8,128)(2,1)}, u32[]{:S(2)}) copy-start(bf16[32,4096]{1,0:T(8,128)(2,1)} %param.9) | copy-start | bytes 786436
  7.2 26.9 %copy-start.1 = (bf16[128,1024]{1,0:T(8,128)(2,1)S(1)}, bf16[128,1024]{1,0:T(8,128)(2,1)}, u32[]{:S(2)}) copy-start(bf16[128,1024]{1,0:T(8,128)(2,1)} %param.13) | copy-start | bytes 786436
  8.9 10.2 %all-to-all-start.2 = ((bf16[32,4,1024]{2,0,1:T(8,128)(2,1)}), bf16[32,4,1024]{2,0,1:T(8,128)(2,1)S(1)}, u32[]{:S(2)}, u32[]{:S(2)}) async-start(bf16[32,4,1024]{2,0,1:T(8,128)(2,1)} %bitcast.107), calls=%async_computation.2 | async-start | bytes 524288 | tf_op jit(solution)/shard_map/all_to_all | solution.py:71
  19.2 9.4 %all-to-all-start = ((bf16[4,32,1024]{2,1,0:T(8,128)(2,1)}), bf16[4,32,1024]{2,1,0:T(8,128)(2,1)S(1)}, u32[]{:S(2)}, u32[]{:S(2)}) async-start(bf16[4,32,1024]{2,1,0:T(8,128)(2,1)} %pad_maximum_fusion), calls=%async_computation | async-start | bytes 524288 | tf_op jit(solution)/shard_map/all_to_all | solution.py:61
  22.6 81.1 %all-gather.6.cloned.1.call-start = ((), (), s32[]{:S(2)}) async-start(), calls=%async_computation.3 | async-start | bytes 4718592 | tf_op jit(solution)/shard_map/all_gather | solution.py:12
  30.4 25.7 %all-to-all-start.1 = ((bf16[32,4,1024]{2,0,1:T(8,128)(2,1)}), bf16[32,4,1024]{2,0,1:T(8,128)(2,1)S(1)}, u32[]{:S(2)}, u32[]{:S(2)}) async-start(bf16[32,4,1024]{2,0,1:T(8,128)(2,1)} %bitcast.108), calls=%async_computation.1 | async-start | bytes 524288 | tf_op jit(solution)/shard_map/all_to_all | solution.py:70
  33.9 153.3 %all-gather.8.cloned.1.call-start = ((), (), s32[]{:S(2)}) async-start(), calls=%async_computation.4 | async-start | bytes 4718592 | tf_op jit(solution)/shard_map/all_gather | solution.py:12
Sparse Core Ops, SparseCore 0:
  29.8 73.7 all-gather.5
  115.8 71.3 all-gather.7
